TPU v7x, 512 devices: a whole 4x4x16 slice. The times are simulated.
512 devices in a mesh: ctx: 64 (over y, z), tp: 8 (over x, core).
Axes of the slice: x: 4, y: 4, z: 16, core: 2. Of those that a mesh axis runs over, the one named last changes fastest.
Arguments:
- query_rows: bfloat16 [32768, 4096], P('ctx', 'tp'), may hold values from -6 to 6
- key_rows: bfloat16 [32768, 4096], P('ctx', 'tp'), may hold values from -0.52734375 to 0.52734375
- value_rows: bfloat16 [32768, 4096], P('ctx', 'tp'), may hold values from -6 to 6
- log_decay: float32 [32, 32768], P('tp', 'ctx'), may hold values from -1 to 0
- norm_gain: float32 [4096], P('tp'), may hold values from 0.25 to 1.75
- out_weight: bfloat16 [4096, 3072], P(None, 'tp'), may hold values from -0.09375 to 0.09375
Outputs:
- projected: bfloat16 [32768, 3072], P('ctx', 'tp')
All inputs are finite; a program needn't handle non-finite values.
Results may differ from a plain program's by a relative error of at most 0.015.
Values may be sent and summed in bfloat16 or wider, within the bound.
A program may use at most 64 MiB of HBM per device.

v0:
```python
import jax
import jax.numpy as jnp
from jax import lax
from jax.sharding import PartitionSpec as P

HEADS = 32
HEAD_DIM = 128
BLOCK = 128


def entering_2(part, axis, combine, identity):
    place = lax.axis_index(axis)
    gathered = jax.tree.map(lambda a: lax.all_gather(a, axis), part)
    state = jax.tree.map(lambda a, e: jnp.zeros_like(a) + jnp.asarray(e, a.dtype), part, identity)

    def one(lap, state):
        return combine(
            state, jax.tree.map(lambda a: lax.dynamic_index_in_dim(a, lap, 0, False), gathered)
        )

    return lax.fori_loop(0, place, one, state)


def chain_combine(earlier, later):
    return (earlier[0] * later[0], later[0][:, None, None] * earlier[1] + later[1])


def incoming_from(shard_decay, shard_state):
    identity = (jnp.ones_like(shard_decay), jnp.zeros_like(shard_state))
    result = entering_2((shard_decay, shard_state), "ctx", chain_combine, identity)
    return result[1]


def split_parts(values):
    high = values.astype(jnp.bfloat16)
    low = (values - high.astype(jnp.float32)).astype(jnp.bfloat16)
    return (high, low)


def split_einsum(form, narrow, wide_first, wide_second):
    if narrow == 0:
        first = jnp.einsum(form, wide_first[0], wide_second, preferred_element_type=jnp.float32)
        second = jnp.einsum(form, wide_first[1], wide_second, preferred_element_type=jnp.float32)
    else:
        first = jnp.einsum(form, wide_first, wide_second[0], preferred_element_type=jnp.float32)
        second = jnp.einsum(form, wide_first, wide_second[1], preferred_element_type=jnp.float32)
    return first + second


def per_device(query_rows, key_rows, value_rows, log_decay, norm_gain, out_weight):
    length = query_rows.shape[0]
    feature_count = query_rows.shape[1]
    head_count = log_decay.shape[0]
    head_width = feature_count // head_count
    blocks = length // BLOCK
    q_block = query_rows.reshape(blocks, BLOCK, head_count, head_width)
    k_block = key_rows.reshape(blocks, BLOCK, head_count, head_width)
    v_block = value_rows.reshape(blocks, BLOCK, head_count, head_width)
    cum = jnp.cumsum(log_decay.reshape(head_count, blocks, BLOCK), axis=-1)
    causal = jnp.arange(BLOCK)[:, None] >= jnp.arange(BLOCK)[None, :]
    spread_log = cum[..., :, None] - cum[..., None, :]
    factor = jnp.where(causal, jnp.exp(jnp.where(causal, spread_log, 0.0)), 0.0)
    scores = jnp.einsum("bthe,bshe->hbts", q_block, k_block, preferred_element_type=jnp.float32)
    weights = (scores * factor).astype(jnp.bfloat16)
    inside_part = jnp.einsum(
        "hbts,bshe->bthe", weights, v_block, preferred_element_type=jnp.float32
    )
    to_end = jnp.transpose(jnp.exp(cum[..., -1:] - cum), (1, 2, 0))
    k_scaled = k_block.astype(jnp.float32) * to_end[..., None]
    block_states = split_einsum("bshe,bshf->bhef", 0, split_parts(k_scaled), v_block)
    block_totals = cum[..., -1]
    block_decay = jnp.exp(block_totals)
    offsets = jnp.cumsum(block_totals, axis=1) - block_totals
    running = jnp.zeros((head_count, head_width, head_width), jnp.float32)
    entering_list = []
    for index_block in range(blocks):
        entering_list.append(running)
        running = block_decay[:, index_block][:, None, None] * running + block_states[index_block]
    entering = jnp.stack(entering_list, axis=0)
    shard_decay = jnp.exp(jnp.sum(block_totals, axis=1))
    growth = jnp.transpose(jnp.exp(cum), (1, 2, 0))[..., None]
    incoming = incoming_from(shard_decay, running)
    entering_all = entering + jnp.transpose(jnp.exp(offsets))[:, :, None, None] * incoming[None]
    carried_part = split_einsum("bthe,bhef->bthf", 1, q_block, split_parts(entering_all)) * growth
    attention = inside_part + carried_part
    attention = attention.reshape(length, feature_count)
    squares = jnp.sum(attention * attention, axis=-1)
    summed = lax.psum(squares, "tp")
    scale = lax.rsqrt(summed / (HEADS * HEAD_DIM) + 1e-06)
    normed = (attention * scale[:, None] * norm_gain).astype(jnp.bfloat16)
    projected = jnp.dot(
        lax.all_gather(normed, "tp", axis=1, tiled=True),
        out_weight,
        preferred_element_type=jnp.float32,
    )
    return projected.astype(jnp.bfloat16)


def solution(mesh):
    in_specs = (
        P("ctx", "tp"),
        P("ctx", "tp"),
        P("ctx", "tp"),
        P("tp", "ctx"),
        P("tp"),
        P(None, "tp"),
    )
    out_specs = P("ctx", "tp")
    return jax.shard_map(
        per_device, mesh=mesh, in_specs=in_specs, out_specs=out_specs, check_vma=False
    )
```

profile of v0, /device:TPU:1, one launch (start us, length us, event | category | flops | bytes accessed | tf_op | source)
XLA Modules:
  0.0 353.3 jit_solution(14344379508308429635)
XLA Ops:
  6.5 0.0 copy-start
  6.5 0.9 reshape.42
  7.4 1.2 reduce_window_sum.24
  8.6 0.2 slice_reduce_fusion
  8.8 0.2 reduce_window_sum.26
  9.0 0.1 bitcast_exponential_fusion
  9.1 2.0 reshape.41
  11.0 2.1 copy.39
  13.1 2.0 reshape.43
  15.0 1.5 fusion.11
  16.5 1.5 convolution_add_fusion.1
  18.1 0.2 slice_reduce_fusion.2
  18.3 1.1 slice_add_fusion
  19.4 0.0 all-gather.4.cloned.1.call-update
  19.4 0.0 all-gather.6.cloned.1.call-start
  19.5 1.3 dynamic-slice
  21.3 0.1 exponential_dynamic-update-slice_fusion
  21.4 123.6 %all-reduce = f32[256]{0:T(256)S(1)} all-reduce(f32[256]{0:T(256)S(1)} %exponential_dynamic-update-slice_fusion), channel_id=2, replica_groups=mesh['ctx'=64,'tp'=8] {'ctx'}, use_global_device_ids=true, to_apply=%add | all-reduce | flops 256 | bytes 2048
  145.0 0.1 reshape.45
  145.1 0.1 copy.43
  145.2 2.0 reshape.40
  147.2 3.1 convolution_bitcast_fusion
  150.3 68.3 %all-gather.4.cloned.1.call-done = f32[64,4,128,128]{3,2,1,0:T(8,128)} async-done(((f32[1,4,128,128]{3,2,1,0:T(8,128)}), f32[64,4,128,128]{3,2,1,0:T(8,128)}) %all-gather.4.cloned.1.call-update) | async-done | bytes 16777232 | tf_op jit(solution)/shard_map/all_gather | solution.py:13
  218.7 0.0 copy-start.1
  218.7 1.9 fusion.27
  220.6 3.3 multiply_reduce_fusion
  223.9 2.5 copy.49
  226.5 12.7 %psum.7 = f32[512]{0:T(512)S(1)} all-reduce(f32[512]{0:T(512)S(1)} %bitcast.40), channel_id=1, replica_groups=mesh['ctx'=64,'tp'=8] {'tp'}, use_global_device_ids=true, to_apply=%region_6.7 | all-reduce | flops 512 | bytes 4096 | tf_op jit(solution)/shard_map/psum | solution.py:88
  239.2 2.2 fusion.5
  241.4 0.0 all-gather.6.cloned.1.call-update
  241.4 99.7 %all-gather.6.cloned.1.call-done = bf16[512,4096]{1,0:T(8,128)(2,1)} async-done(((bf16[512,512]{1,0:T(8,128)(2,1)}), bf16[512,4096]{1,0:T(8,128)(2,1)}) %all-gather.6.cloned.1.call-update) | async-done | bytes 4194320 | tf_op jit(solution)/shard_map/all_gather | solution.py:92
  341.2 5.3 %convolution_convert_fusion = bf16[512,384]{1,0:T(8,128)(2,1)} fusion(bf16[512,4096]{1,0:T(8,128)(2,1)} %all-gather.6.cloned.1.call-done, bf16[4096,384]{1,0:T(8,128)(2,1)S(1)} %copy-done), kind=kOutput, calls=%fused_computation.10 | convolution fusion | flops 1610809344 | bytes 7733248 | tf_op jit(solution)/shard_map/dot_general | solution.py:91
  (13 shorter events, 0.1 us)
Async XLA Ops:
  6.5 334.6 %copy-start = (bf16[4096,384]{1,0:T(8,128)(2,1)S(1)}, bf16[4096,384]{1,0:T(8,128)(2,1)}, u32[]{:S(2)}) copy-start(bf16[4096,384]{1,0:T(8,128)(2,1)} %param.13) | copy-start | bytes 9437188
  6.5 212.1 %all-gather.4.cloned.1.call-start = ((), (), s32[]{:S(2)}) async-start(), calls=%async_computation | async-start | bytes 17039360 | tf_op jit(solution)/shard_map/all_gather | solution.py:13
  19.4 321.8 %all-gather.6.cloned.1.call-start = ((), (), s32[]{:S(2)}) async-start(), calls=%async_computation.1 | async-start | bytes 4718592 | tf_op jit(solution)/shard_map/all_gather | solution.py:92
  218.7 20.6 %copy-start.1 = (f32[512]{0:T(512)S(1)}, f32[512]{0:T(512)}, u32[]{:S(2)}) copy-start(f32[512]{0:T(512)} %param.12) | copy-start | bytes 6148
Sparse Core Ops, SparseCore 0:
  19.5 199.0 all-gather.3
  241.6 99.5 all-gather.5
where the time goes:
time: 356 us; the launch traced here: 353 us
  waiting for transfers between devices  168 us (47%)
  blocking collectives  136 us (38%)
  matrix products  16.6 us (5%)
  between operations  14.1 us (4%)
  local copies, waits for them, and re-layouts  13 us (4%)
  other arithmetic  5.13 us (1%)
    unnamed x1, blocking collectives  124 us
    all_gather x1, waiting for transfers between devices, per_device(): lax.all_gather(normed, 'tp', axis=1, tiled=True)  99.7 us
    all_gather x1, waiting for transfers between devices, entering_2(): gathered = jax.tree.map(lambda a: lax.all_gather(a, axis), part)  68.3 us
    psum x1, blocking collectives, per_device(): summed = lax.psum(squares, 'tp')  12.7 us
  transfers between devices with their start and end apart: 2, of which 2 were waited for; matrix products, arithmetic and copies ran while one was open for 2% of the time, Pallas kernels for 0%

commit v1 on v0

--- a/solution.py
+++ b/solution.py
@@ -1,11 +1,26 @@
+import functools
 import jax
 import jax.numpy as jnp
 from jax import lax
 from jax.sharding import PartitionSpec as P
+from jax.lax import all_to_all, psum
 
 HEADS = 32
 HEAD_DIM = 128
 BLOCK = 128
+
+
+def make_outputs(original, d_out):
+    arrivals = []
+    for _ in range(psum(1, axis_name="tp")):
+        arrivals.append(original)
+    everything = all_to_all(
+        jnp.stack(arrivals, axis=0), axis_name="tp", split_axis=0, concat_axis=0
+    )
+    return jnp.concatenate(everything, axis=d_out)
+
+
+cut_the_limits = functools.partial(make_outputs, d_out=1)
 
 
 def entering_2(part, axis, combine, identity):
@@ -88,11 +103,7 @@
     summed = lax.psum(squares, "tp")
     scale = lax.rsqrt(summed / (HEADS * HEAD_DIM) + 1e-06)
     normed = (attention * scale[:, None] * norm_gain).astype(jnp.bfloat16)
-    projected = jnp.dot(
-        lax.all_gather(normed, "tp", axis=1, tiled=True),
-        out_weight,
-        preferred_element_type=jnp.float32,
-    )
+    projected = jnp.dot(cut_the_limits(normed), out_weight, preferred_element_type=jnp.float32)
     return projected.astype(jnp.bfloat16)
 
 

time: 356 us -> 371 us (1.042)
  the two profiles are of different devices: /device:TPU:1 before, /device:TPU:504 now
where the time goes in v1:
time: 371 us; the launch traced here: 368 us
  blocking collectives  206 us (56%)
  other arithmetic  72 us (19%)
  waiting for transfers between devices  42.4 us (11%)
  local copies, waits for them, and re-layouts  17.2 us (5%)
  matrix products  14.4 us (4%)
  between operations  14.1 us (4%)
    unnamed x1, blocking collectives  139 us
    add x63, other arithmetic, chain_combine(): later[0][:, None, None] * earlier[1] + later[1]  66.9 us
    all_to_all x1, blocking collectives, make_outputs(): all_to_all(jnp.stack(arrivals, axis=0), axis_name='tp', split_axis=0, con...  52.8 us
    all_gather x1, waiting for transfers between devices, entering_2(): gathered = jax.tree.map(lambda a: lax.all_gather(a, axis), part)  42.4 us
    psum x1, blocking collectives, per_device(): summed = lax.psum(squares, 'tp')  14.4 us
  transfers between devices with their start and end apart: 1, of which 1 were waited for; matrix products, arithmetic and copies ran while one was open for 2% of the time, Pallas kernels for 0%

profile of v1, /device:TPU:504, one launch (start us, length us, event | category | flops | bytes accessed | tf_op | source)
XLA Modules:
  0.0 368.4 jit_solution(3828141726856711832)
XLA Ops:
  7.4 1.2 reduce_window_sum.24
  9.1 2.0 reshape.65
  11.0 2.1 copy.40
  13.1 2.0 reshape.67
  15.0 1.5 fusion.11
  16.5 1.5 convolution_add_fusion.1
  18.3 1.1 slice_add_fusion
  19.4 1.3 dynamic-slice
  21.4 138.9 %all-reduce = f32[256]{0:T(256)S(1)} all-reduce(f32[256]{0:T(256)S(1)} %exponential_dynamic-update-slice_fusion), channel_id=2, replica_groups=mesh['ctx'=64,'tp'=8] {'ctx'}, use_global_device_ids=true, to_apply=%add | all-reduce | flops 256 | bytes 2048
  160.5 2.0 reshape.64
  162.5 3.1 convolution_bitcast_fusion
  165.6 42.4 %all-gather.3.cloned.1.call-done = f32[64,4,128,128]{3,2,1,0:T(8,128)} async-done(((f32[1,4,128,128]{3,2,1,0:T(8,128)}), f32[64,4,128,128]{3,2,1,0:T(8,128)}) %all-gather.3.cloned.1.call-update) | async-done | bytes 16777232 | tf_op jit(solution)/shard_map/all_gather | solution.py:28
  208.0 69.8 %while.12 = (s32[]{:T(128)}, f32[4,128,128]{2,1,0:T(8,128)S(1)}, s32[]{:T(128)}, f32[64,4]{1,0:T(8,128)S(1)}, f32[64,4,128,128]{3,2,1,0:T(8,128)}, /*index=5*/s32[]{:T(128)}, s32[]{:T(128)}, s32[]{:T(128)}) while((s32[]{:T(128)}, f32[4,128,128]{2,1,0:T(8,128)S(1)}, s32[]{:T(128)}, f32[64,4]{1,0:T(8,128)S(1)}, f32[64,4,128,128]{3,2,1,0:T(8,128)}, ...), condition=%wide.region_4.5_spmd, body=%wide.region_3.4_spmd.sunk | while | flops 131077 | bytes 786607 | solution.py:36
  208.0 1.1 bitcast_add_fusion.2
  209.1 1.1 bitcast_add_fusion.2
  210.2 1.1 bitcast_add_fusion.2
  211.4 1.1 bitcast_add_fusion.2
  213.6 1.1 bitcast_add_fusion.2
  214.7 1.1 bitcast_add_fusion.2
  215.8 1.1 bitcast_add_fusion.2
  216.9 1.1 bitcast_add_fusion.2
  218.0 1.1 bitcast_add_fusion.2
  219.1 1.1 bitcast_add_fusion.2
  277.8 1.9 fusion.27
  279.8 3.3 multiply_reduce_fusion
  283.1 2.5 copy.50
  285.6 14.4 %psum.7 = f32[512]{0:T(512)S(1)} all-reduce(f32[512]{0:T(512)S(1)} %bitcast.44), channel_id=1, replica_groups=mesh['ctx'=64,'tp'=8] {'tp'}, use_global_device_ids=true, to_apply=%region_6.7 | all-reduce | flops 512 | bytes 4096 | tf_op jit(solution)/shard_map/psum | solution.py:103
  300.0 2.2 fusion.5
  302.2 2.0 copy.51
  304.3 1.4 stack.5
  305.7 52.8 %all_to_all.5 = bf16[8,512,512]{1,2,0:T(8,128)(2,1)S(1)} all-to-all(bf16[8,512,512]{1,2,0:T(8,128)(2,1)S(1)} %stack.5), channel_id=1, replica_groups=mesh['ctx'=64,'tp'=8] {'tp'}, dimensions={0} | all-to-all | bytes 8388608 | tf_op jit(solution)/shard_map/all_to_all | solution.py:17
  358.5 3.1 convolution_convert_fusion
  (139 shorter events, 58.9 us)
Async XLA Ops:
  6.5 351.9 %copy-start = (bf16[4096,384]{1,0:T(8,128)(2,1)S(1)}, bf16[4096,384]{1,0:T(8,128)(2,1)}, u32[]{:S(2)}) copy-start(bf16[4096,384]{1,0:T(8,128)(2,1)} %param.13) | copy-start | bytes 9437188
  6.5 201.4 %all-gather.3.cloned.1.call-start = ((), (), s32[]{:S(2)}) async-start(), calls=%async_computation.1 | async-start | bytes 17039360 | tf_op jit(solution)/shard_map/all_gather | solution.py:28
  277.8 22.2 %copy-start.1 = (f32[512]{0:T(512)S(1)}, f32[512]{0:T(512)}, u32[]{:S(2)}) copy-start(f32[512]{0:T(512)} %param.12) | copy-start | bytes 6148
Sparse Core Ops, SparseCore 0:
  19.5 188.4 all-gather.2
